TPU v7x, 32 devices: a whole 2x2x4 slice. The times are simulated.
32 devices in a mesh: gx: 4 (over y, x), gy: 8 (over z, core).
Axes of the slice: x: 2, y: 2, z: 4, core: 2. Of those that a mesh axis runs over, the one named last changes fastest.
Arguments:
- right_side: float32 [8, 3, 64, 1024], P(None, None, 'gx', 'gy'), may hold values from -50 to 50
- first_guess: float32 [8, 3, 64, 1024], P(None, None, 'gx', 'gy'), may hold values from -3 to 3
- diag_block: bfloat16 [8, 3, 3, 64, 1024], P(None, None, None, 'gx', 'gy'), may hold values from -2.41 to 12
- mobility: bfloat16 [8, 3, 3, 64, 1024], P(None, None, None, 'gx', 'gy'), may hold values from -1 to 1.21
- face_trans: bfloat16 [6, 8, 64, 1024], P(None, None, 'gx', 'gy'), may hold values from 0.19921875 to 1
- column_inverse: bfloat16 [4, 6, 6, 64, 1024], P(None, None, None, 'gx', 'gy'), may hold values from -0.061 to 0.201
- perf_cell: int32 [32, 32, 40], P(('gx', 'gy')), may hold values from 0 to 16383, as said below
- perf_slot: int32 [32, 32, 40], P(('gx', 'gy')), may hold values from 0 to 1024, as said below
- well_in: float32 [3, 32768], P(None, ('gx', 'gy')), may hold values from -4 to 4
- well_out: float32 [3, 32768], P(None, ('gx', 'gy')), may hold values from -4 to 4
- well_inverse: float32 [256, 128, 128], P(('gx', 'gy')), may hold values from -1 to 1
Outputs:
- solution: float32 [8, 3, 64, 1024], P(None, None, 'gx', 'gy')
- residual: float32 [8, 3, 64, 1024], P(None, None, 'gx', 'gy')
Inputs may be any that keep to these rules, and one draw needn't show every extreme that they name: `perf_cell`: entry [s, d, q] is a local cell number of device s's tile, the cell of slot q from device s to owner d; the slot's segment is perf_slot[d, s, q]; slots that perf_slot marks empty carry an arbitrary cell. `perf_slot`: entry [d, s, q] is w * 128 + g when slot q from device s carries segment g of owner d's local well w, and 1024 when the slot is empty. Each segment of an owner appears at most once; the segments of a well that appear are 0 to n - 1 for its padded count n of 1 to 128. Every pair (d, s) has at most 40 live slots and some pair has exactly 40; in every draw some owner has all 1024 segments live.
All inputs are finite; a program needn't handle non-finite values.
Results may differ from a plain program's by a relative error of at most 0.0003.
Values sent between devices are 32-bit elements; how exact they have to be, the bound alone decides.
No kernel may reach another device: no remote copies, remote signals or barrier semaphores. Data moves between devices by JAX's collectives and lax.ppermute only.
A program may use at most 128 MiB of HBM per device.

v0:
```python
import jax
import jax.numpy as jnp
from jax import lax
from jax.sharding import PartitionSpec as P

ITERS = 2


def padded_2(block, sides, width):
    for axis, dim in sides:
        count = lax.axis_size(axis)
        forward = [(i, i + 1) for i in range(count - 1)]
        backward = [(target, source) for source, target in forward]
        low = lax.ppermute(
            lax.slice_in_dim(block, block.shape[dim] - width, None, axis=dim), axis, forward
        )
        high = lax.ppermute(lax.slice_in_dim(block, 0, width, axis=dim), axis, backward)
        block = jnp.concatenate([low, block, high], axis=dim)
    return block


def couple(mixing, vector):
    summed = mixing[:, :, 0].astype(jnp.float32) * vector[:, 0:1]
    summed = summed + mixing[:, :, 1].astype(jnp.float32) * vector[:, 1:2]
    summed = summed + mixing[:, :, 2].astype(jnp.float32) * vector[:, 2:3]
    return summed


def stencil(vector, extended, diag_block, face_trans):
    factor = face_trans.astype(jnp.float32)[:, :, None]
    interior = extended[:, :, 1:-1, 1:-1]
    zero_layer = jnp.zeros_like(interior[:1])
    under_layer = jnp.concatenate([zero_layer, interior[:-1]], axis=0)
    over_layer = jnp.concatenate([interior[1:], zero_layer], axis=0)
    beside = factor[0] * extended[:, :, :-2, 1:-1]
    beside = beside + factor[1] * extended[:, :, 2:, 1:-1]
    beside = beside + factor[2] * extended[:, :, 1:-1, :-2]
    beside = beside + factor[3] * extended[:, :, 1:-1, 2:]
    beside = beside + factor[4] * under_layer
    beside = beside + factor[5] * over_layer
    return couple(diag_block, vector) - beside


def precondition(vector, column_inverse):
    layers, comps, tile_rows, tile_cols = vector.shape
    paired = vector.reshape(layers // 2, 6, tile_rows, tile_cols)
    result = column_inverse[:, :, 0].astype(jnp.float32) * paired[:, 0:1]
    for member in range(1, 6):
        result = (
            result
            + column_inverse[:, :, member].astype(jnp.float32) * paired[:, member : member + 1]
        )
    return result.reshape(vector.shape)


def per_device(
    right_side,
    first_guess,
    diag_block,
    mobility,
    face_trans,
    column_inverse,
    perf_cell,
    perf_slot,
    well_in,
    well_out,
    well_inverse,
):
    layers, comps, tile_rows, tile_cols = right_side.shape
    tile_area = tile_rows * tile_cols
    cell_ids = perf_cell[0]
    targets = perf_slot[0]
    layer_idx = cell_ids // tile_area
    column_idx = cell_ids % tile_area
    well_count = well_inverse.shape[0]
    seg_count = well_inverse.shape[1]
    per_owner = well_count * seg_count
    pad_in = jnp.concatenate([well_in, jnp.zeros((3, 1), jnp.float32)], axis=1)
    pad_out = jnp.concatenate([well_out, jnp.zeros((3, 1), jnp.float32)], axis=1)

    def solve_wells(rate):
        totals = jnp.zeros((per_owner + 1,), jnp.float32).at[targets].add(rate)
        seg_rate = jnp.einsum(
            "wgh,wh->wg",
            well_inverse,
            totals[:per_owner].reshape(well_count, seg_count),
            precision=lax.Precision.HIGHEST,
        )
        padded = jnp.concatenate([seg_rate.reshape(-1), jnp.zeros((1,), jnp.float32)])
        return padded[targets]

    def well_term(vector):
        flattened = vector.reshape(layers, comps, tile_area)
        values = flattened[layer_idx, :, column_idx]
        outgoing = jnp.moveaxis(values, 2, 0)
        arrived = lax.all_to_all(outgoing, ("gx", "gy"), split_axis=1, concat_axis=1, tiled=True)
        coeff_in = pad_in[:, targets]
        rate = coeff_in[0] * arrived[0] + coeff_in[1] * arrived[1] + coeff_in[2] * arrived[2]
        back = solve_wells(rate)
        terms = lax.all_to_all(
            pad_out[:, targets] * back[None], ("gx", "gy"), split_axis=1, concat_axis=1, tiled=True
        )
        scattered = (
            jnp.zeros((layers, comps, tile_area), jnp.float32)
            .at[layer_idx, :, column_idx]
            .add(jnp.moveaxis(terms, 0, 2))
        )
        return scattered.reshape(vector.shape)

    def apply_operator(vector):
        flux = couple(mobility, vector)
        extended = padded_2(flux, (("gx", 2), ("gy", 3)), 1)
        return stencil(vector, extended, diag_block, face_trans) - well_term(vector)

    iterate = first_guess
    residual = right_side - apply_operator(iterate)
    shadow = residual
    inner_now = lax.psum(jnp.sum(shadow * residual), ("gx", "gy"))
    search = residual
    for iteration in range(ITERS):
        search_hat = precondition(search, column_inverse)
        applied = apply_operator(search_hat)
        projected = lax.psum(jnp.sum(shadow * applied), ("gx", "gy"))
        step_size = inner_now / projected
        halfway = residual - step_size * applied
        halfway_hat = precondition(halfway, column_inverse)
        response = apply_operator(halfway_hat)
        cross_term, self_term, shadow_term = lax.psum(
            (jnp.sum(response * halfway), jnp.sum(response * response), jnp.sum(shadow * response)),
            ("gx", "gy"),
        )
        smoothing = cross_term / self_term
        iterate = iterate + step_size * search_hat + smoothing * halfway_hat
        residual = halfway - smoothing * response
        if iteration + 1 < ITERS:
            inner_next = inner_now - step_size * projected - smoothing * shadow_term
            momentum = inner_next / inner_now * (step_size / smoothing)
            search = residual + momentum * (search - smoothing * applied)
            inner_now = inner_next
    return (iterate, right_side - apply_operator(iterate))


def solution(mesh):
    in_specs = (
        P(None, None, "gx", "gy"),
        P(None, None, "gx", "gy"),
        P(None, None, None, "gx", "gy"),
        P(None, None, None, "gx", "gy"),
        P(None, None, "gx", "gy"),
        P(None, None, None, "gx", "gy"),
        P(("gx", "gy"), None, None),
        P(("gx", "gy"), None, None),
        P(None, ("gx", "gy")),
        P(None, ("gx", "gy")),
        P(("gx", "gy"), None, None),
    )
    out_specs = (P(None, None, "gx", "gy"), P(None, None, "gx", "gy"))
    return jax.shard_map(
        per_device, mesh=mesh, in_specs=in_specs, out_specs=out_specs, check_vma=False
    )
```

profile of v0, /device:TPU:0, one launch (start us, length us, event | category | flops | bytes accessed | tf_op | source)
XLA Modules:
  0.0 751.7 jit_solution(8360309148296932770)
XLA Ops:
  1.6 5.7 copy.372
  7.4 9.6 %gather_fusion.2 = f32[1280,3]{1,0:T(8,128)S(1)} fusion(f32[8,3,2048]{1,2,0:T(8,128)} %bitcast.585, s32[1280]{0:T(1024)S(1)} %reshape.496), kind=kCustom, calls=%fused_computation.2 | custom fusion | bytes 40960 | tf_op jit(solution)/shard_map/gather | solution.py:94
  17.8 7.3 all-to-all-start
  49.9 7.3 scatter_custom_fusion
  58.2 7.1 gather_fusion.3
  66.1 6.4 all-to-all-start.1
  73.1 6.7 all-to-all-done.1
  81.0 13.1 %scatter_custom_fusion.6 = f32[3,16384]{0,1:T(8,128)} fusion(s32[1280]{0:T(1024)S(1)} %reshape.628, f32[1280,3]{1,0:T(8,128)} %bitcast.636, f32[]{:T(128)} %constant.32.clone.1), kind=kCustom, calls=%fused_computation.36 | custom fusion | flops 3840 | bytes 197120
  94.2 5.9 copy.377
  113.1 5.6 copy.398
  118.7 12.7 %gather_fusion.4 = f32[1280,3]{1,0:T(8,128)} fusion(f32[8,3,2048]{1,2,0:T(8,128)} %copy.398, s32[1280]{0:T(1024)S(1)} %reshape.496), kind=kCustom, calls=%fused_computation.4 | custom fusion | bytes 40960 | tf_op jit(solution)/shard_map/gather | solution.py:94
  147.1 7.5 scatter_custom_fusion.1
  155.5 10.0 %gather_fusion.5 = f32[1280]{0:T(1024)} fusion(f32[1025]{0:T(1024)S(1)} %pad_maximum_fusion.58, s32[2048]{0:T(1024)} %copy-done.22), kind=kCustom, calls=%fused_computation.5 | custom fusion | bytes 15360 | tf_op jit(solution)/shard_map/gather | solution.py:90
  168.4 6.0 all-to-all-start.3
  176.1 5.6 all-to-all-done.3
  183.7 12.9 %scatter_custom_fusion.7 = f32[3,16384]{0,1:T(8,128)} fusion(s32[1280]{0:T(1024)} %copy-done.70, f32[1280,3]{1,0:T(8,128)} %bitcast.637, f32[]{:T(128)} %constant.32.clone.1), kind=kCustom, calls=%fused_computation.34 | custom fusion | flops 3840 | bytes 197120
  196.6 5.9 copy.403
  206.1 38.8 %all-reduce.16 = (f32[]{:T(128)}, f32[]{:T(128)}) all-reduce(f32[]{:T(128)} %get-tuple-element.18, f32[]{:T(128)} %get-tuple-element.17), channel_id=1, replica_groups=mesh['gx'=4,'gy'=8] {'gx','gy'}, use_global_device_ids=true, to_apply=%region_3.4 | all-reduce | flops 2 | bytes 16 | tf_op jit(solution)/shard_map/psum | solution.py:118
  252.2 5.4 collective-permute-start.8
  258.9 5.6 copy.418
  264.5 12.7 %gather_fusion.6 = f32[1280,3]{1,0:T(8,128)} fusion(f32[8,3,2048]{1,2,0:T(8,128)} %copy.418, s32[1280]{0:T(1024)S(1)} %reshape.496), kind=kCustom, calls=%fused_computation.6 | custom fusion | bytes 40960 | tf_op jit(solution)/shard_map/gather | solution.py:94
  293.6 7.5 scatter_custom_fusion.2
  302.0 10.0 %gather_fusion.7 = f32[1280]{0:T(1024)} fusion(f32[1025]{0:T(1024)S(1)} %pad_maximum_fusion.57, s32[2048]{0:T(1024)} %copy-done.22), kind=kCustom, calls=%fused_computation.7 | custom fusion | bytes 15360 | tf_op jit(solution)/shard_map/gather | solution.py:90
  314.9 6.0 all-to-all-start.5
  330.1 12.9 %scatter_custom_fusion.8 = f32[3,16384]{0,1:T(8,128)} fusion(s32[1280]{0:T(1024)} %copy-done.70, f32[1280,3]{1,0:T(8,128)} %bitcast.638, f32[]{:T(128)} %constant.32.clone.1), kind=kCustom, calls=%fused_computation.32 | custom fusion | flops 3840 | bytes 197120
  343.0 5.9 copy.423
  352.5 38.6 %all-reduce.15 = (f32[]{:T(128)}, f32[]{:T(128)}, f32[]{:T(128)}) all-reduce(f32[]{:T(128)} %get-tuple-element.16, f32[]{:T(128)} %get-tuple-element.15, f32[]{:T(128)} %get-tuple-element.14), channel_id=1, replica_groups=mesh['gx'=4,'gy'=8] {'gx','gy'}, use_global_device_ids=true, to_apply=%region_11.12 | all-reduce | flops 3 | bytes 24 | tf_op jit(solution)/shard_map/psum | solution.py:128
  401.7 5.4 collective-permute-start.12
  408.5 5.6 copy.437
  414.1 12.7 %gather_fusion.8 = f32[1280,3]{1,0:T(8,128)} fusion(f32[8,3,2048]{1,2,0:T(8,128)} %copy.437, s32[1280]{0:T(1024)S(1)} %reshape.496), kind=kCustom, calls=%fused_computation.8 | custom fusion | bytes 40960 | tf_op jit(solution)/shard_map/gather | solution.py:94
  443.0 7.5 scatter_custom_fusion.3
  451.5 10.0 %gather_fusion.9 = f32[1280]{0:T(1024)} fusion(f32[1025]{0:T(1024)S(1)} %pad_maximum_fusion.56, s32[2048]{0:T(1024)} %copy-done.22), kind=kCustom, calls=%fused_computation.9 | custom fusion | bytes 15360 | tf_op jit(solution)/shard_map/gather | solution.py:90
  464.3 6.0 all-to-all-start.7
  472.1 5.6 all-to-all-done.7
  479.7 12.9 %scatter_custom_fusion.9 = f32[3,16384]{0,1:T(8,128)} fusion(s32[1280]{0:T(1024)} %copy-done.70, f32[1280,3]{1,0:T(8,128)} %bitcast.639, f32[]{:T(128)} %constant.32.clone.1), kind=kCustom, calls=%fused_computation.30 | custom fusion | flops 3840 | bytes 197120
  492.6 5.9 copy.442
  501.9 38.4 %psum.61 = f32[]{:T(128)} all-reduce(f32[]{:T(128)} %get-tuple-element.26), channel_id=1, replica_groups=mesh['gx'=4,'gy'=8] {'gx','gy'}, use_global_device_ids=true, to_apply=%region_19.20 | all-reduce | flops 1 | bytes 8 | tf_op jit(solution)/shard_map/psum | solution.py:123
  555.9 9.6 %gather_fusion.10 = f32[1280,3]{1,0:T(8,128)S(1)} fusion(f32[8,3,2048]{1,2,0:T(8,128)} %copy.456, s32[1280]{0:T(1024)S(1)} %reshape.496), kind=kCustom, calls=%fused_computation.10 | custom fusion | bytes 40960 | tf_op jit(solution)/shard_map/gather | solution.py:94
  578.3 7.5 scatter_custom_fusion.4
  586.8 7.1 gather_fusion.11
  600.2 6.7 all-to-all-done.9
  608.2 12.9 %scatter_custom_fusion.10 = f32[3,16384]{0,1:T(8,128)} fusion(s32[1280]{0:T(1024)} %copy-done.70, f32[1280,3]{1,0:T(8,128)} %bitcast.640, f32[]{:T(128)} %constant.32.clone.1), kind=kCustom, calls=%fused_computation.28 | custom fusion | flops 3840 | bytes 197120
  628.7 38.6 %all-reduce.14 = (f32[]{:T(128)}, f32[]{:T(128)}) all-reduce(f32[]{:T(128)} %get-tuple-element.13, f32[]{:T(128)} %get-tuple-element.12), channel_id=1, replica_groups=mesh['gx'=4,'gy'=8] {'gx','gy'}, use_global_device_ids=true, to_apply=%region_23.24 | all-reduce | flops 2 | bytes 16 | tf_op jit(solution)/shard_map/psum | solution.py:128
  679.7 9.6 %gather_fusion.12 = f32[1280,3]{1,0:T(8,128)S(1)} fusion(f32[8,3,2048]{1,2,0:T(8,128)} %bitcast.586, s32[1280]{0:T(1024)S(1)} %reshape.496), kind=kCustom, calls=%fused_computation.12 | custom fusion | bytes 40960 | tf_op jit(solution)/shard_map/gather | solution.py:94
  702.2 7.5 scatter_custom_fusion.5
  710.7 7.1 gather_fusion.13
  724.0 6.7 all-to-all-done.11
  731.0 12.8 %scatter_custom_fusion.11 = f32[3,16384]{0,1:T(8,128)} fusion(s32[1280]{0:T(1024)} %copy-done.70, f32[1280,3]{1,0:T(8,128)S(1)} %bitcast.635, f32[]{:T(128)} %constant.32.clone.1), kind=kCustom, calls=%fused_computation.26 | custom fusion | flops 3840 | bytes 197120
  (401 shorter events, 223.8 us)
Async XLA Ops:
  0.6 56.6 %copy-start = (f32[8,128,128]{2,1,0:T(8,128)S(1)}, f32[8,128,128]{2,1,0:T(8,128)}, u32[]{:S(2)}) copy-start(f32[8,128,128]{2,1,0:T(8,128)} %param.21) | copy-start | bytes 1572868
  17.8 31.9 %all-to-all-start = ((f32[3,32,40]{2,0,1:T(4,128)}), f32[3,32,40]{2,0,1:T(4,128)S(1)}, u32[]{:S(2)}, u32[]{:S(2)}) async-start(f32[3,32,40]{2,0,1:T(4,128)} %bitcast.22), calls=%async_computation | async-start | bytes 131072 | tf_op jit(solution)/shard_map/all_to_all | solution.py:96
  25.4 32.8 %copy-start.11 = (f32[8,3,16,128]{3,2,0,1:T(8,128)}, f32[8,3,16,128]{3,2,0,1:T(8,128)S(1)}, u32[]{:S(2)}) copy-start(f32[8,3,16,128]{3,2,0,1:T(8,128)S(1)} %fusion.39) | copy-start | bytes 589828
  25.4 18.2 %collective-permute-start.1 = (f32[8,3,1,128]{3,2,0,1:T(1,128)S(1)}, f32[8,3,1,128]{3,2,0,1:T(1,128)S(1)}, u32[]{:S(2)}, u32[]{:S(2)}) collective-permute-start(f32[8,3,1,128]{3,2,0,1:T(1,128)S(1)} %get-tuple-element.122), channel_id=1, source_target_pairs={{8,0},{16,8},{24,16},{9,1},{17,9},{25,17},{10,2},{18,10},{26,18},{... | collective-permute-start | bytes 36872 | tf_op jit(solution)/shard_map/ppermute | solution.py:17
  26.7 16.9 %collective-permute-start = (f32[8,3,1,128]{3,2,0,1:T(1,128)S(1)}, f32[8,3,1,128]{3,2,0,1:T(1,128)S(1)}, u32[]{:S(2)}, u32[]{:S(2)}) collective-permute-start(f32[8,3,1,128]{3,2,0,1:T(1,128)S(1)} %get-tuple-element.121), channel_id=1, source_target_pairs={{0,8},{8,16},{16,24},{1,9},{9,17},{17,25},{2,10},{10,18},{18,26},{... | collective-permute-start | bytes 36872 | tf_op jit(solution)/shard_map/ppermute | solution.py:14
  32.5 32.8 %copy-start.66 = (s32[1280]{0:T(1024)}, s32[1280]{0:T(1024)S(1)}, u32[]{:S(2)}) copy-start(s32[1280]{0:T(1024)S(1)} %reshape.482) | copy-start | bytes 15364
  44.6 55.5 %collective-permute-start.3 = (f32[8,3,18,1]{3,2,0,1:T(8,128)}, f32[8,3,18,1]{3,2,0,1:T(8,128)}, u32[]{:S(2)}, u32[]{:S(2)}) collective-permute-start(f32[8,3,18,1]{3,2,0,1:T(8,128)} %get-tuple-element.56), channel_id=1, source_target_pairs={{1,0},{2,1},{3,2},{4,3},{5,4},{6,5},{7,6},{9,8},{10,9},{11,10},{12... | collective-permute-start | bytes 5192 | tf_op jit(solution)/shard_map/ppermute | solution.py:17
  45.9 54.2 %collective-permute-start.2 = (f32[8,3,18,1]{3,2,0,1:T(8,128)}, f32[8,3,18,1]{3,2,0,1:T(8,128)}, u32[]{:S(2)}, u32[]{:S(2)}) collective-permute-start(f32[8,3,18,1]{3,2,0,1:T(8,128)} %get-tuple-element.55), channel_id=1, source_target_pairs={{0,1},{1,2},{2,3},{3,4},{4,5},{5,6},{6,7},{8,9},{9,10},{10,11},{11... | collective-permute-start | bytes 5192 | tf_op jit(solution)/shard_map/ppermute | solution.py:14
  66.1 13.8 %all-to-all-start.1 = ((f32[3,32,40]{2,0,1:T(4,128)}), f32[3,32,40]{2,0,1:T(4,128)S(1)}, u32[]{:S(2)}, u32[]{:S(2)}) async-start(f32[3,32,40]{2,0,1:T(4,128)} %multiply_bitcast_fusion.5), calls=%async_computation.1 | async-start | bytes 131072 | tf_op jit(solution)/shard_map/all_to_all | solution.py:100
  105.1 31.6 %collective-permute-start.5 = (f32[8,3,1,128]{3,2,0,1:T(1,128)}, f32[8,3,1,128]{3,2,0,1:T(1,128)}, u32[]{:S(2)}, u32[]{:S(2)}) collective-permute-start(f32[8,3,1,128]{3,2,0,1:T(1,128)} %get-tuple-element.107), channel_id=1, source_target_pairs={{8,0},{16,8},{24,16},{9,1},{17,9},{25,17},{10,2},{18,10},{26,18},{... | collective-permute-start | bytes 36872 | tf_op jit(solution)/shard_map/ppermute | solution.py:17
  106.4 30.3 %collective-permute-start.4 = (f32[8,3,1,128]{3,2,0,1:T(1,128)}, f32[8,3,1,128]{3,2,0,1:T(1,128)}, u32[]{:S(2)}, u32[]{:S(2)}) collective-permute-start(f32[8,3,1,128]{3,2,0,1:T(1,128)} %get-tuple-element.106), channel_id=1, source_target_pairs={{0,8},{8,16},{16,24},{1,9},{9,17},{17,25},{2,10},{10,18},{18,26},{... | collective-permute-start | bytes 36872 | tf_op jit(solution)/shard_map/ppermute | solution.py:14
  133.4 10.5 %all-to-all-start.2 = ((f32[3,32,40]{2,0,1:T(4,128)}), f32[3,32,40]{2,0,1:T(4,128)}, u32[]{:S(2)}, u32[]{:S(2)}) async-start(f32[3,32,40]{2,0,1:T(4,128)} %bitcast.707), calls=%async_computation.2 | async-start | bytes 131072 | tf_op jit(solution)/shard_map/all_to_all | solution.py:96
  138.6 63.9 %collective-permute-start.7 = (f32[8,3,18,1]{3,2,0,1:T(8,128)}, f32[8,3,18,1]{3,2,0,1:T(8,128)}, u32[]{:S(2)}, u32[]{:S(2)}) collective-permute-start(f32[8,3,18,1]{3,2,0,1:T(8,128)} %get-tuple-element.51), channel_id=1, source_target_pairs={{1,0},{2,1},{3,2},{4,3},{5,4},{6,5},{7,6},{9,8},{10,9},{11,10},{12... | collective-permute-start | bytes 5192 | tf_op jit(solution)/shard_map/ppermute | solution.py:17
  139.9 62.6 %collective-permute-start.6 = (f32[8,3,18,1]{3,2,0,1:T(8,128)}, f32[8,3,18,1]{3,2,0,1:T(8,128)}, u32[]{:S(2)}, u32[]{:S(2)}) collective-permute-start(f32[8,3,18,1]{3,2,0,1:T(8,128)} %get-tuple-element.50), channel_id=1, source_target_pairs={{0,1},{1,2},{2,3},{3,4},{4,5},{5,6},{6,7},{8,9},{9,10},{10,11},{11... | collective-permute-start | bytes 5192 | tf_op jit(solution)/shard_map/ppermute | solution.py:14
  168.4 13.3 %all-to-all-start.3 = ((f32[3,32,40]{2,0,1:T(4,128)}), f32[3,32,40]{2,0,1:T(4,128)}, u32[]{:S(2)}, u32[]{:S(2)}) async-start(f32[3,32,40]{2,0,1:T(4,128)} %multiply_bitcast_fusion.4), calls=%async_computation.3 | async-start | bytes 131072 | tf_op jit(solution)/shard_map/all_to_all | solution.py:100
  250.8 32.3 %collective-permute-start.9 = (f32[8,3,1,128]{3,2,0,1:T(1,128)}, f32[8,3,1,128]{3,2,0,1:T(1,128)}, u32[]{:S(2)}, u32[]{:S(2)}) collective-permute-start(f32[8,3,1,128]{3,2,0,1:T(1,128)} %get-tuple-element.94), channel_id=1, source_target_pairs={{8,0},{16,8},{24,16},{9,1},{17,9},{25,17},{10,2},{18,10},{26,18},{... | collective-permute-start | bytes 36872 | tf_op jit(solution)/shard_map/ppermute | solution.py:17
  252.2 31.0 %collective-permute-start.8 = (f32[8,3,1,128]{3,2,0,1:T(1,128)}, f32[8,3,1,128]{3,2,0,1:T(1,128)}, u32[]{:S(2)}, u32[]{:S(2)}) collective-permute-start(f32[8,3,1,128]{3,2,0,1:T(1,128)} %get-tuple-element.93), channel_id=1, source_target_pairs={{0,8},{8,16},{16,24},{1,9},{9,17},{17,25},{2,10},{10,18},{18,26},{... | collective-permute-start | bytes 36872 | tf_op jit(solution)/shard_map/ppermute | solution.py:14
  279.2 11.2 %all-to-all-start.4 = ((f32[3,32,40]{2,0,1:T(4,128)}), f32[3,32,40]{2,0,1:T(4,128)}, u32[]{:S(2)}, u32[]{:S(2)}) async-start(f32[3,32,40]{2,0,1:T(4,128)} %bitcast.708), calls=%async_computation.4 | async-start | bytes 131072 | tf_op jit(solution)/shard_map/all_to_all | solution.py:96
  285.1 63.8 %collective-permute-start.11 = (f32[8,3,18,1]{3,2,0,1:T(8,128)}, f32[8,3,18,1]{3,2,0,1:T(8,128)}, u32[]{:S(2)}, u32[]{:S(2)}) collective-permute-start(f32[8,3,18,1]{3,2,0,1:T(8,128)} %get-tuple-element.49), channel_id=1, source_target_pairs={{1,0},{2,1},{3,2},{4,3},{5,4},{6,5},{7,6},{9,8},{10,9},{11,10},{12... | collective-permute-start | bytes 5192 | tf_op jit(solution)/shard_map/ppermute | solution.py:17
  286.4 62.5 %collective-permute-start.10 = (f32[8,3,18,1]{3,2,0,1:T(8,128)}, f32[8,3,18,1]{3,2,0,1:T(8,128)}, u32[]{:S(2)}, u32[]{:S(2)}) collective-permute-start(f32[8,3,18,1]{3,2,0,1:T(8,128)} %get-tuple-element.48), channel_id=1, source_target_pairs={{0,1},{1,2},{2,3},{3,4},{4,5},{5,6},{6,7},{8,9},{9,10},{10,11},{11... | collective-permute-start | bytes 5192 | tf_op jit(solution)/shard_map/ppermute | solution.py:14
  314.9 13.2 %all-to-all-start.5 = ((f32[3,32,40]{2,0,1:T(4,128)}), f32[3,32,40]{2,0,1:T(4,128)}, u32[]{:S(2)}, u32[]{:S(2)}) async-start(f32[3,32,40]{2,0,1:T(4,128)} %multiply_bitcast_fusion.3), calls=%async_computation.5 | async-start | bytes 131072 | tf_op jit(solution)/shard_map/all_to_all | solution.py:100
  400.4 32.3 %collective-permute-start.13 = (f32[8,3,1,128]{3,2,0,1:T(1,128)}, f32[8,3,1,128]{3,2,0,1:T(1,128)}, u32[]{:S(2)}, u32[]{:S(2)}) collective-permute-start(f32[8,3,1,128]{3,2,0,1:T(1,128)} %get-tuple-element.81), channel_id=1, source_target_pairs={{8,0},{16,8},{24,16},{9,1},{17,9},{25,17},{10,2},{18,10},{26,18},{... | collective-permute-start | bytes 36872 | tf_op jit(solution)/shard_map/ppermute | solution.py:17
  401.7 31.0 %collective-permute-start.12 = (f32[8,3,1,128]{3,2,0,1:T(1,128)}, f32[8,3,1,128]{3,2,0,1:T(1,128)}, u32[]{:S(2)}, u32[]{:S(2)}) collective-permute-start(f32[8,3,1,128]{3,2,0,1:T(1,128)} %get-tuple-element.80), channel_id=1, source_target_pairs={{0,8},{8,16},{16,24},{1,9},{9,17},{17,25},{2,10},{10,18},{18,26},{... | collective-permute-start | bytes 36872 | tf_op jit(solution)/shard_map/ppermute | solution.py:14
  428.8 11.1 %all-to-all-start.6 = ((f32[3,32,40]{2,0,1:T(4,128)}), f32[3,32,40]{2,0,1:T(4,128)}, u32[]{:S(2)}, u32[]{:S(2)}) async-start(f32[3,32,40]{2,0,1:T(4,128)} %bitcast.709), calls=%async_computation.6 | async-start | bytes 131072 | tf_op jit(solution)/shard_map/all_to_all | solution.py:96
  434.6 63.8 %collective-permute-start.15 = (f32[8,3,18,1]{3,2,0,1:T(8,128)}, f32[8,3,18,1]{3,2,0,1:T(8,128)}, u32[]{:S(2)}, u32[]{:S(2)}) collective-permute-start(f32[8,3,18,1]{3,2,0,1:T(8,128)} %get-tuple-element.47), channel_id=1, source_target_pairs={{1,0},{2,1},{3,2},{4,3},{5,4},{6,5},{7,6},{9,8},{10,9},{11,10},{12... | collective-permute-start | bytes 5192 | tf_op jit(solution)/shard_map/ppermute | solution.py:17
  435.9 62.6 %collective-permute-start.14 = (f32[8,3,18,1]{3,2,0,1:T(8,128)}, f32[8,3,18,1]{3,2,0,1:T(8,128)}, u32[]{:S(2)}, u32[]{:S(2)}) collective-permute-start(f32[8,3,18,1]{3,2,0,1:T(8,128)} %get-tuple-element.46), channel_id=1, source_target_pairs={{0,1},{1,2},{2,3},{3,4},{4,5},{5,6},{6,7},{8,9},{9,10},{10,11},{11... | collective-permute-start | bytes 5192 | tf_op jit(solution)/shard_map/ppermute | solution.py:14
  464.3 13.3 %all-to-all-start.7 = ((f32[3,32,40]{2,0,1:T(4,128)}), f32[3,32,40]{2,0,1:T(4,128)}, u32[]{:S(2)}, u32[]{:S(2)}) async-start(f32[3,32,40]{2,0,1:T(4,128)} %multiply_bitcast_fusion.2), calls=%async_computation.7 | async-start | bytes 131072 | tf_op jit(solution)/shard_map/all_to_all | solution.py:100
  544.3 26.5 %collective-permute-start.17 = (f32[8,3,1,128]{3,2,0,1:T(1,128)S(1)}, f32[8,3,1,128]{3,2,0,1:T(1,128)S(1)}, u32[]{:S(2)}, u32[]{:S(2)}) collective-permute-start(f32[8,3,1,128]{3,2,0,1:T(1,128)S(1)} %get-tuple-element.70), channel_id=1, source_target_pairs={{8,0},{16,8},{24,16},{9,1},{17,9},{25,17},{10,2},{18,10},{26,18},{... | collective-permute-start | bytes 36872 | tf_op jit(solution)/shard_map/ppermute | solution.py:17
  545.6 25.2 %collective-permute-start.16 = (f32[8,3,1,128]{3,2,0,1:T(1,128)S(1)}, f32[8,3,1,128]{3,2,0,1:T(1,128)S(1)}, u32[]{:S(2)}, u32[]{:S(2)}) collective-permute-start(f32[8,3,1,128]{3,2,0,1:T(1,128)S(1)} %get-tuple-element.69), channel_id=1, source_target_pairs={{0,8},{8,16},{16,24},{1,9},{9,17},{17,25},{2,10},{10,18},{18,26},{... | collective-permute-start | bytes 36872 | tf_op jit(solution)/shard_map/ppermute | solution.py:14
  551.2 35.6 %copy-start.23 = (s32[2048]{0:T(1024)S(1)}, s32[2048]{0:T(1024)}, u32[]{:S(2)}) copy-start(s32[2048]{0:T(1024)} %copy-done.22) | copy-start | bytes 24580
  566.4 11.8 %all-to-all-start.8 = ((f32[3,32,40]{2,0,1:T(4,128)}), f32[3,32,40]{2,0,1:T(4,128)S(1)}, u32[]{:S(2)}, u32[]{:S(2)}) async-start(f32[3,32,40]{2,0,1:T(4,128)} %bitcast.150), calls=%async_computation.8 | async-start | bytes 131072 | tf_op jit(solution)/shard_map/all_to_all | solution.py:96
  571.8 54.6 %collective-permute-start.19 = (f32[8,3,18,1]{3,2,0,1:T(8,128)}, f32[8,3,18,1]{3,2,0,1:T(8,128)}, u32[]{:S(2)}, u32[]{:S(2)}) collective-permute-start(f32[8,3,18,1]{3,2,0,1:T(8,128)} %get-tuple-element.45), channel_id=1, source_target_pairs={{1,0},{2,1},{3,2},{4,3},{5,4},{6,5},{7,6},{9,8},{10,9},{11,10},{12... | collective-permute-start | bytes 5192 | tf_op jit(solution)/shard_map/ppermute | solution.py:17
  573.1 53.3 %collective-permute-start.18 = (f32[8,3,18,1]{3,2,0,1:T(8,128)}, f32[8,3,18,1]{3,2,0,1:T(8,128)}, u32[]{:S(2)}, u32[]{:S(2)}) collective-permute-start(f32[8,3,18,1]{3,2,0,1:T(8,128)} %get-tuple-element.44), channel_id=1, source_target_pairs={{0,1},{1,2},{2,3},{3,4},{4,5},{5,6},{6,7},{8,9},{9,10},{10,11},{11... | collective-permute-start | bytes 5192 | tf_op jit(solution)/shard_map/ppermute | solution.py:14
  594.6 12.2 %all-to-all-start.9 = ((f32[3,32,40]{2,0,1:T(4,128)}), f32[3,32,40]{2,0,1:T(4,128)S(1)}, u32[]{:S(2)}, u32[]{:S(2)}) async-start(f32[3,32,40]{2,0,1:T(4,128)} %multiply_bitcast_fusion.1), calls=%async_computation.9 | async-start | bytes 131072 | tf_op jit(solution)/shard_map/all_to_all | solution.py:100
  608.1 60.6 %copy-start.27 = (f32[8,3,16,128]{3,2,0,1:T(8,128)S(1)}, f32[8,3,16,128]{3,2,0,1:T(8,128)}, u32[]{:S(2)}) copy-start(f32[8,3,16,128]{3,2,0,1:T(8,128)} %copy-done.26) | copy-start | bytes 589828
  608.1 60.6 %copy-start.29 = (f32[8,3,16,128]{3,2,0,1:T(8,128)S(1)}, f32[8,3,16,128]{3,2,0,1:T(8,128)}, u32[]{:S(2)}) copy-start(f32[8,3,16,128]{3,2,0,1:T(8,128)} %copy-done.28) | copy-start | bytes 589828
  608.1 60.6 %copy-start.31 = (f32[8,3,16,128]{3,2,0,1:T(8,128)S(1)}, f32[8,3,16,128]{3,2,0,1:T(8,128)}, u32[]{:S(2)}) copy-start(f32[8,3,16,128]{3,2,0,1:T(8,128)} %copy-done.30) | copy-start | bytes 589828
  608.1 60.6 %copy-start.33 = (f32[8,3,16,128]{3,2,0,1:T(8,128)S(1)}, f32[8,3,16,128]{3,2,0,1:T(8,128)}, u32[]{:S(2)}) copy-start(f32[8,3,16,128]{3,2,0,1:T(8,128)} %copy-done.32) | copy-start | bytes 589828
  608.1 60.6 %copy-start.37 = (f32[8,3,16,128]{3,2,1,0:T(8,128)S(1)}, f32[8,3,16,128]{3,2,1,0:T(8,128)}, u32[]{:S(2)}) copy-start(f32[8,3,16,128]{3,2,1,0:T(8,128)} %param.12) | copy-start | bytes 589828
  621.1 47.7 %copy-start.6 = (bf16[8,3,1,16,128]{4,3,2,1,0:T(8,128)(2,1)S(1)}, bf16[8,3,1,16,128]{4,3,2,1,0:T(8,128)(2,1)}, u32[]{:S(2)}) copy-start(bf16[8,3,1,16,128]{4,3,2,1,0:T(8,128)(2,1)} %copy-done.5) | copy-start | bytes 294916
  621.1 47.7 %copy-start.8 = (bf16[8,3,1,16,128]{4,3,2,1,0:T(8,128)(2,1)S(1)}, bf16[8,3,1,16,128]{4,3,2,1,0:T(8,128)(2,1)}, u32[]{:S(2)}) copy-start(bf16[8,3,1,16,128]{4,3,2,1,0:T(8,128)(2,1)} %copy-done.7) | copy-start | bytes 294916
  621.1 47.8 %copy-start.10 = (bf16[8,3,1,16,128]{4,3,2,1,0:T(8,128)(2,1)S(1)}, bf16[8,3,1,16,128]{4,3,2,1,0:T(8,128)(2,1)}, u32[]{:S(2)}) copy-start(bf16[8,3,1,16,128]{4,3,2,1,0:T(8,128)(2,1)} %copy-done.9) | copy-start | bytes 294916
  669.0 25.7 %collective-permute-start.21 = (f32[8,3,1,128]{3,2,0,1:T(1,128)S(1)}, f32[8,3,1,128]{3,2,0,1:T(1,128)S(1)}, u32[]{:S(2)}, u32[]{:S(2)}) collective-permute-start(f32[8,3,1,128]{3,2,0,1:T(1,128)S(1)} %get-tuple-element.63), channel_id=1, source_target_pairs={{8,0},{16,8},{24,16},{9,1},{17,9},{25,17},{10,2},{18,10},{26,18},{... | collective-permute-start | bytes 36872 | tf_op jit(solution)/shard_map/ppermute | solution.py:17
  670.3 24.4 %collective-permute-start.20 = (f32[8,3,1,128]{3,2,0,1:T(1,128)S(1)}, f32[8,3,1,128]{3,2,0,1:T(1,128)S(1)}, u32[]{:S(2)}, u32[]{:S(2)}) collective-permute-start(f32[8,3,1,128]{3,2,0,1:T(1,128)S(1)} %get-tuple-element.62), channel_id=1, source_target_pairs={{0,8},{8,16},{16,24},{1,9},{9,17},{17,25},{2,10},{10,18},{18,26},{... | collective-permute-start | bytes 36872 | tf_op jit(solution)/shard_map/ppermute | solution.py:14
  690.2 11.8 %all-to-all-start.10 = ((f32[3,32,40]{2,0,1:T(4,128)}), f32[3,32,40]{2,0,1:T(4,128)S(1)}, u32[]{:S(2)}, u32[]{:S(2)}) async-start(f32[3,32,40]{2,0,1:T(4,128)} %bitcast.167), calls=%async_computation.10 | async-start | bytes 131072 | tf_op jit(solution)/shard_map/all_to_all | solution.py:96
  695.6 53.4 %collective-permute-start.23 = (f32[8,3,18,1]{3,2,0,1:T(8,128)}, f32[8,3,18,1]{3,2,0,1:T(8,128)}, u32[]{:S(2)}, u32[]{:S(2)}) collective-permute-start(f32[8,3,18,1]{3,2,0,1:T(8,128)} %get-tuple-element.43), channel_id=1, source_target_pairs={{1,0},{2,1},{3,2},{4,3},{5,4},{6,5},{7,6},{9,8},{10,9},{11,10},{12... | collective-permute-start | bytes 5192 | tf_op jit(solution)/shard_map/ppermute | solution.py:17
  696.9 52.1 %collective-permute-start.22 = (f32[8,3,18,1]{3,2,0,1:T(8,128)}, f32[8,3,18,1]{3,2,0,1:T(8,128)}, u32[]{:S(2)}, u32[]{:S(2)}) collective-permute-start(f32[8,3,18,1]{3,2,0,1:T(8,128)} %get-tuple-element.42), channel_id=1, source_target_pairs={{0,1},{1,2},{2,3},{3,4},{4,5},{5,6},{6,7},{8,9},{9,10},{10,11},{11... | collective-permute-start | bytes 5192 | tf_op jit(solution)/shard_map/ppermute | solution.py:14
  718.5 12.2 %all-to-all-start.11 = ((f32[3,32,40]{2,0,1:T(4,128)}), f32[3,32,40]{2,0,1:T(4,128)S(1)}, u32[]{:S(2)}, u32[]{:S(2)}) async-start(f32[3,32,40]{2,0,1:T(4,128)} %multiply_bitcast_fusion), calls=%async_computation.11 | async-start | bytes 131072 | tf_op jit(solution)/shard_map/all_to_all | solution.py:100
  (61 other events, 901.6 us)
where the time goes:
time: 764 us; the launch traced here: 752 us
  local copies, waits for them, and re-layouts  242 us (32%)
  other arithmetic  169 us (22%)
  blocking collectives  154 us (20%)
  starting transfers between devices  129 us (17%)
  waiting for transfers between devices  38.7 us (5%)
  between operations  13.2 us (2%)
    unnamed x9, other arithmetic  77.9 us
    psum x2, blocking collectives, per_device(): lax.psum((jnp.sum(response * halfway), jnp.sum(response * response), jnp....  77.2 us
    gather x12, local copies, waits for them, and re-layouts, well_term(): values = flattened[layer_idx, :, column_idx]  75.5 us
    gather x12, local copies, waits for them, and re-layouts, solve_wells(): return padded[targets]  55.7 us
    ppermute x12, starting transfers between devices, padded_2(): lax.ppermute(lax.slice_in_dim(block, block.shape[dim] - width, None, axis...  52.9 us
    unnamed x176, local copies, waits for them, and re-layouts  45.4 us
    scatter-add x6, other arithmetic, solve_wells(): totals = jnp.zeros((per_owner + 1,), jnp.float32).at[targets].add(rate)  44.8 us
    psum x1, blocking collectives, per_device(): inner_now = lax.psum(jnp.sum(shadow * residual), ('gx', 'gy'))  38.8 us
  transfers between devices with their start and end apart: 36, of which 11 were waited for; matrix products, arithmetic and copies ran while one was open for 49% of the time, Pallas kernels for 0%

commit v1 on v0

--- a/solution.py
+++ b/solution.py
@@ -97,8 +97,16 @@
         coeff_in = pad_in[:, targets]
         rate = coeff_in[0] * arrived[0] + coeff_in[1] * arrived[1] + coeff_in[2] * arrived[2]
         back = solve_wells(rate)
-        terms = lax.all_to_all(
-            pad_out[:, targets] * back[None], ("gx", "gy"), split_axis=1, concat_axis=1, tiled=True
+        terms = jnp.concatenate(
+            lax.all_to_all(
+                jnp.stack(
+                    jnp.split(pad_out[:, targets] * back[None], lax.axis_size(("gx", "gy")), axis=1)
+                ),
+                ("gx", "gy"),
+                0,
+                0,
+            ),
+            axis=1,
         )
         scattered = (
             jnp.zeros((layers, comps, tile_area), jnp.float32)

time: 764 us -> 787 us (1.030)
  local copies, waits for them, and re-layouts: 242 us -> 268 us
    another operation x0 -> x24, local copies, waits for them, and re-layouts: none -> 26.8 us  [well_term(): jnp.stack(jnp.split(pad_out[:, targets] * back[None], lax.axis_size(('gx'...]
  transfers between devices with their start and end apart: 36 -> 36, of which waited for: 11 -> 11; matrix products, arithmetic and copies ran while one was open for 49% -> 50% of each run, Pallas kernels for 0% -> 0%
where the time goes in v1:
time: 787 us; the launch traced here: 774 us
  local copies, waits for them, and re-layouts  268 us (34%)
  other arithmetic  165 us (21%)
  blocking collectives  154 us (20%)
  starting transfers between devices  129 us (16%)
  waiting for transfers between devices  38.9 us (5%)
  between operations  13.1 us (2%)
    unnamed x9, other arithmetic  78.1 us
    psum x2, blocking collectives, per_device(): lax.psum((jnp.sum(response * halfway), jnp.sum(response * response), jnp....  77.2 us
    gather x12, local copies, waits for them, and re-layouts, well_term(): values = flattened[layer_idx, :, column_idx]  75.6 us
    gather x12, local copies, waits for them, and re-layouts, solve_wells(): return padded[targets]  55.7 us
    ppermute x12, starting transfers between devices, padded_2(): lax.ppermute(lax.slice_in_dim(block, block.shape[dim] - width, None, axis...  52.8 us
    unnamed x176, local copies, waits for them, and re-layouts  45.4 us
    scatter-add x6, other arithmetic, solve_wells(): totals = jnp.zeros((per_owner + 1,), jnp.float32).at[targets].add(rate)  44.8 us
    psum x1, blocking collectives, per_device(): inner_now = lax.psum(jnp.sum(shadow * residual), ('gx', 'gy'))  38.8 us
  transfers between devices with their start and end apart: 36, of which 11 were waited for; matrix products, arithmetic and copies ran while one was open for 50% of the time, Pallas kernels for 0%

profile of v1, /device:TPU:0, one launch (start us, length us, event | category | flops | bytes accessed | tf_op | source)
XLA Modules:
  0.0 774.3 jit_solution(2962961475071824413)
XLA Ops:
  1.6 5.7 copy.640
  7.4 9.6 %gather_fusion.2 = f32[1280,3]{1,0:T(8,128)S(1)} fusion(f32[8,3,2048]{1,2,0:T(8,128)} %bitcast.1005, s32[1280]{0:T(1024)S(1)} %reshape.544), kind=kCustom, calls=%fused_computation.2 | custom fusion | bytes 40960 | tf_op jit(solution)/shard_map/gather | solution.py:94
  17.8 7.3 all-to-all-start
  50.0 7.3 scatter_custom_fusion
  58.3 7.1 gather_fusion.3
  66.4 6.4 all-to-all-start.1
  73.5 6.7 all-to-all-done.1
  81.3 13.2 %scatter_custom_fusion.6 = f32[3,16384]{0,1:T(8,128)} fusion(s32[1280]{0:T(1024)S(1)} %reshape.676, f32[1280,3]{1,0:T(8,128)} %bitcast.1056, f32[]{:T(128)} %constant.32.clone.1), kind=kCustom, calls=%fused_computation.36 | custom fusion | flops 3840 | bytes 197120
  94.4 5.9 copy.646
  113.3 5.6 copy.667
  118.9 12.7 %gather_fusion.4 = f32[1280,3]{1,0:T(8,128)} fusion(f32[8,3,2048]{1,2,0:T(8,128)} %copy.667, s32[1280]{0:T(1024)S(1)} %reshape.544), kind=kCustom, calls=%fused_computation.4 | custom fusion | bytes 40960 | tf_op jit(solution)/shard_map/gather | solution.py:94
  147.4 7.5 scatter_custom_fusion.1
  155.9 10.0 %gather_fusion.5 = f32[1280]{0:T(1024)} fusion(f32[1025]{0:T(1024)S(1)} %pad_maximum_fusion.58, s32[2048]{0:T(1024)} %copy-done.22), kind=kCustom, calls=%fused_computation.5 | custom fusion | bytes 15360 | tf_op jit(solution)/shard_map/gather | solution.py:90
  176.2 5.8 all-to-all-start.3
  183.7 5.5 all-to-all-done.3
  191.2 13.0 %scatter_custom_fusion.7 = f32[3,16384]{0,1:T(8,128)} fusion(s32[1280]{0:T(1024)} %copy-done.70, f32[1280,3]{1,0:T(8,128)} %bitcast.1057, f32[]{:T(128)} %constant.32.clone.1), kind=kCustom, calls=%fused_computation.34 | custom fusion | flops 3840 | bytes 197120
  204.2 5.9 copy.673
  213.6 38.8 %all-reduce.16 = (f32[]{:T(128)}, f32[]{:T(128)}) all-reduce(f32[]{:T(128)} %get-tuple-element.22, f32[]{:T(128)} %get-tuple-element.21), channel_id=1, replica_groups=mesh['gx'=4,'gy'=8] {'gx','gy'}, use_global_device_ids=true, to_apply=%region_3.4 | all-reduce | flops 2 | bytes 16 | tf_op jit(solution)/shard_map/psum | solution.py:126
  259.6 5.4 collective-permute-start.8
  266.4 5.6 copy.688
  272.0 12.7 %gather_fusion.6 = f32[1280,3]{1,0:T(8,128)} fusion(f32[8,3,2048]{1,2,0:T(8,128)} %copy.688, s32[1280]{0:T(1024)S(1)} %reshape.544), kind=kCustom, calls=%fused_computation.6 | custom fusion | bytes 40960 | tf_op jit(solution)/shard_map/gather | solution.py:94
  301.0 7.5 scatter_custom_fusion.2
  309.4 10.0 %gather_fusion.7 = f32[1280]{0:T(1024)} fusion(f32[1025]{0:T(1024)S(1)} %pad_maximum_fusion.57, s32[2048]{0:T(1024)} %copy-done.22), kind=kCustom, calls=%fused_computation.7 | custom fusion | bytes 15360 | tf_op jit(solution)/shard_map/gather | solution.py:90
  329.7 5.9 all-to-all-start.5
  344.9 13.0 %scatter_custom_fusion.8 = f32[3,16384]{0,1:T(8,128)} fusion(s32[1280]{0:T(1024)} %copy-done.70, f32[1280,3]{1,0:T(8,128)} %bitcast.1058, f32[]{:T(128)} %constant.32.clone.1), kind=kCustom, calls=%fused_computation.32 | custom fusion | flops 3840 | bytes 197120
  357.9 5.9 copy.694
  367.3 38.5 %all-reduce.15 = (f32[]{:T(128)}, f32[]{:T(128)}, f32[]{:T(128)}) all-reduce(f32[]{:T(128)} %get-tuple-element.20, f32[]{:T(128)} %get-tuple-element.19, f32[]{:T(128)} %get-tuple-element.18), channel_id=1, replica_groups=mesh['gx'=4,'gy'=8] {'gx','gy'}, use_global_device_ids=true, to_apply=%region_11.12 | all-reduce | flops 3 | bytes 24 | tf_op jit(solution)/shard_map/psum | solution.py:136
  416.4 5.4 collective-permute-start.12
  423.2 5.6 copy.708
  428.8 12.7 %gather_fusion.8 = f32[1280,3]{1,0:T(8,128)} fusion(f32[8,3,2048]{1,2,0:T(8,128)} %copy.708, s32[1280]{0:T(1024)S(1)} %reshape.544), kind=kCustom, calls=%fused_computation.8 | custom fusion | bytes 40960 | tf_op jit(solution)/shard_map/gather | solution.py:94
  458.0 7.5 scatter_custom_fusion.3
  466.4 10.0 %gather_fusion.9 = f32[1280]{0:T(1024)} fusion(f32[1025]{0:T(1024)S(1)} %pad_maximum_fusion.56, s32[2048]{0:T(1024)} %copy-done.22), kind=kCustom, calls=%fused_computation.9 | custom fusion | bytes 15360 | tf_op jit(solution)/shard_map/gather | solution.py:90
  486.7 5.8 all-to-all-start.7
  494.3 5.5 all-to-all-done.7
  501.8 13.0 %scatter_custom_fusion.9 = f32[3,16384]{0,1:T(8,128)} fusion(s32[1280]{0:T(1024)} %copy-done.70, f32[1280,3]{1,0:T(8,128)} %bitcast.1059, f32[]{:T(128)} %constant.32.clone.1), kind=kCustom, calls=%fused_computation.30 | custom fusion | flops 3840 | bytes 197120
  514.7 5.9 copy.714
  524.1 38.5 %psum.61 = f32[]{:T(128)} all-reduce(f32[]{:T(128)} %get-tuple-element.30), channel_id=1, replica_groups=mesh['gx'=4,'gy'=8] {'gx','gy'}, use_global_device_ids=true, to_apply=%region_19.20 | all-reduce | flops 1 | bytes 8 | tf_op jit(solution)/shard_map/psum | solution.py:131
  578.1 9.6 %gather_fusion.10 = f32[1280,3]{1,0:T(8,128)S(1)} fusion(f32[8,3,2048]{1,2,0:T(8,128)} %copy.728, s32[1280]{0:T(1024)S(1)} %reshape.544), kind=kCustom, calls=%fused_computation.10 | custom fusion | bytes 40960 | tf_op jit(solution)/shard_map/gather | solution.py:94
  600.5 7.5 scatter_custom_fusion.4
  609.0 7.1 gather_fusion.11
  622.6 6.6 all-to-all-done.9
  630.5 13.0 %scatter_custom_fusion.10 = f32[3,16384]{0,1:T(8,128)} fusion(s32[1280]{0:T(1024)} %copy-done.70, f32[1280,3]{1,0:T(8,128)} %bitcast.1060, f32[]{:T(128)} %constant.32.clone.1), kind=kCustom, calls=%fused_computation.28 | custom fusion | flops 3840 | bytes 197120
  651.2 38.6 %all-reduce.14 = (f32[]{:T(128)}, f32[]{:T(128)}) all-reduce(f32[]{:T(128)} %get-tuple-element.17, f32[]{:T(128)} %get-tuple-element.16), channel_id=1, replica_groups=mesh['gx'=4,'gy'=8] {'gx','gy'}, use_global_device_ids=true, to_apply=%region_23.24 | all-reduce | flops 2 | bytes 16 | tf_op jit(solution)/shard_map/psum | solution.py:136
  702.3 9.6 %gather_fusion.12 = f32[1280,3]{1,0:T(8,128)S(1)} fusion(f32[8,3,2048]{1,2,0:T(8,128)} %bitcast.1006, s32[1280]{0:T(1024)S(1)} %reshape.544), kind=kCustom, calls=%fused_computation.12 | custom fusion | bytes 40960 | tf_op jit(solution)/shard_map/gather | solution.py:94
  724.7 7.5 scatter_custom_fusion.5
  733.2 7.1 gather_fusion.13
  746.7 6.6 all-to-all-done.11
  753.6 12.9 %scatter_custom_fusion.11 = f32[3,16384]{0,1:T(8,128)} fusion(s32[1280]{0:T(1024)} %copy-done.70, f32[1280,3]{1,0:T(8,128)S(1)} %bitcast.1055, f32[]{:T(128)} %constant.32.clone.1), kind=kCustom, calls=%fused_computation.26 | custom fusion | flops 3840 | bytes 197120
  (425 shorter events, 246.9 us)
Async XLA Ops:
  0.6 56.7 %copy-start = (f32[8,128,128]{2,1,0:T(8,128)S(1)}, f32[8,128,128]{2,1,0:T(8,128)}, u32[]{:S(2)}) copy-start(f32[8,128,128]{2,1,0:T(8,128)} %param.21) | copy-start | bytes 1572868
  17.8 31.9 %all-to-all-start = ((f32[3,32,40]{2,0,1:T(4,128)}), f32[3,32,40]{2,0,1:T(4,128)S(1)}, u32[]{:S(2)}, u32[]{:S(2)}) async-start(f32[3,32,40]{2,0,1:T(4,128)} %bitcast.22), calls=%async_computation | async-start | bytes 131072 | tf_op jit(solution)/shard_map/all_to_all | solution.py:96
  25.4 32.9 %copy-start.11 = (f32[8,3,16,128]{3,2,0,1:T(8,128)}, f32[8,3,16,128]{3,2,0,1:T(8,128)S(1)}, u32[]{:S(2)}) copy-start(f32[8,3,16,128]{3,2,0,1:T(8,128)S(1)} %fusion.39) | copy-start | bytes 589828
  25.4 18.3 %collective-permute-start.1 = (f32[8,3,1,128]{3,2,0,1:T(1,128)S(1)}, f32[8,3,1,128]{3,2,0,1:T(1,128)S(1)}, u32[]{:S(2)}, u32[]{:S(2)}) collective-permute-start(f32[8,3,1,128]{3,2,0,1:T(1,128)S(1)} %get-tuple-element.126), channel_id=1, source_target_pairs={{8,0},{16,8},{24,16},{9,1},{17,9},{25,17},{10,2},{18,10},{26,18},{... | collective-permute-start | bytes 36872 | tf_op jit(solution)/shard_map/ppermute | solution.py:17
  26.7 17.0 %collective-permute-start = (f32[8,3,1,128]{3,2,0,1:T(1,128)S(1)}, f32[8,3,1,128]{3,2,0,1:T(1,128)S(1)}, u32[]{:S(2)}, u32[]{:S(2)}) collective-permute-start(f32[8,3,1,128]{3,2,0,1:T(1,128)S(1)} %get-tuple-element.125), channel_id=1, source_target_pairs={{0,8},{8,16},{16,24},{1,9},{9,17},{17,25},{2,10},{10,18},{18,26},{... | collective-permute-start | bytes 36872 | tf_op jit(solution)/shard_map/ppermute | solution.py:14
  32.5 32.9 %copy-start.66 = (s32[1280]{0:T(1024)}, s32[1280]{0:T(1024)S(1)}, u32[]{:S(2)}) copy-start(s32[1280]{0:T(1024)S(1)} %reshape.530) | copy-start | bytes 15364
  44.7 55.6 %collective-permute-start.3 = (f32[8,3,18,1]{3,2,0,1:T(8,128)}, f32[8,3,18,1]{3,2,0,1:T(8,128)}, u32[]{:S(2)}, u32[]{:S(2)}) collective-permute-start(f32[8,3,18,1]{3,2,0,1:T(8,128)} %get-tuple-element.60), channel_id=1, source_target_pairs={{1,0},{2,1},{3,2},{4,3},{5,4},{6,5},{7,6},{9,8},{10,9},{11,10},{12... | collective-permute-start | bytes 5192 | tf_op jit(solution)/shard_map/ppermute | solution.py:17
  46.0 54.3 %collective-permute-start.2 = (f32[8,3,18,1]{3,2,0,1:T(8,128)}, f32[8,3,18,1]{3,2,0,1:T(8,128)}, u32[]{:S(2)}, u32[]{:S(2)}) collective-permute-start(f32[8,3,18,1]{3,2,0,1:T(8,128)} %get-tuple-element.59), channel_id=1, source_target_pairs={{0,1},{1,2},{2,3},{3,4},{4,5},{5,6},{6,7},{8,9},{9,10},{10,11},{11... | collective-permute-start | bytes 5192 | tf_op jit(solution)/shard_map/ppermute | solution.py:14
  66.4 13.8 %all-to-all-start.1 = ((f32[32,3,1,40]{3,2,1,0:T(1,128)}), f32[32,3,1,40]{3,2,1,0:T(1,128)S(1)}, u32[]{:S(2)}, u32[]{:S(2)}) async-start(f32[32,3,1,40]{3,2,1,0:T(1,128)} %copy.643), calls=%async_computation.1 | async-start | bytes 98304 | tf_op jit(solution)/shard_map/all_to_all | solution.py:101
  105.4 31.5 %collective-permute-start.5 = (f32[8,3,1,128]{3,2,0,1:T(1,128)}, f32[8,3,1,128]{3,2,0,1:T(1,128)}, u32[]{:S(2)}, u32[]{:S(2)}) collective-permute-start(f32[8,3,1,128]{3,2,0,1:T(1,128)} %get-tuple-element.111), channel_id=1, source_target_pairs={{8,0},{16,8},{24,16},{9,1},{17,9},{25,17},{10,2},{18,10},{26,18},{... | collective-permute-start | bytes 36872 | tf_op jit(solution)/shard_map/ppermute | solution.py:17
  106.7 30.3 %collective-permute-start.4 = (f32[8,3,1,128]{3,2,0,1:T(1,128)}, f32[8,3,1,128]{3,2,0,1:T(1,128)}, u32[]{:S(2)}, u32[]{:S(2)}) collective-permute-start(f32[8,3,1,128]{3,2,0,1:T(1,128)} %get-tuple-element.110), channel_id=1, source_target_pairs={{0,8},{8,16},{16,24},{1,9},{9,17},{17,25},{2,10},{10,18},{18,26},{... | collective-permute-start | bytes 36872 | tf_op jit(solution)/shard_map/ppermute | solution.py:14
  133.6 10.6 %all-to-all-start.2 = ((f32[3,32,40]{2,0,1:T(4,128)}), f32[3,32,40]{2,0,1:T(4,128)}, u32[]{:S(2)}, u32[]{:S(2)}) async-start(f32[3,32,40]{2,0,1:T(4,128)} %bitcast.1127), calls=%async_computation.2 | async-start | bytes 131072 | tf_op jit(solution)/shard_map/all_to_all | solution.py:96
  138.8 71.2 %collective-permute-start.7 = (f32[8,3,18,1]{3,2,0,1:T(8,128)}, f32[8,3,18,1]{3,2,0,1:T(8,128)}, u32[]{:S(2)}, u32[]{:S(2)}) collective-permute-start(f32[8,3,18,1]{3,2,0,1:T(8,128)} %get-tuple-element.55), channel_id=1, source_target_pairs={{1,0},{2,1},{3,2},{4,3},{5,4},{6,5},{7,6},{9,8},{10,9},{11,10},{12... | collective-permute-start | bytes 5192 | tf_op jit(solution)/shard_map/ppermute | solution.py:17
  140.1 70.0 %collective-permute-start.6 = (f32[8,3,18,1]{3,2,0,1:T(8,128)}, f32[8,3,18,1]{3,2,0,1:T(8,128)}, u32[]{:S(2)}, u32[]{:S(2)}) collective-permute-start(f32[8,3,18,1]{3,2,0,1:T(8,128)} %get-tuple-element.54), channel_id=1, source_target_pairs={{0,1},{1,2},{2,3},{3,4},{4,5},{5,6},{6,7},{8,9},{9,10},{10,11},{11... | collective-permute-start | bytes 5192 | tf_op jit(solution)/shard_map/ppermute | solution.py:14
  176.2 13.1 %all-to-all-start.3 = ((f32[32,3,1,40]{3,2,1,0:T(1,128)}), f32[32,3,1,40]{3,2,1,0:T(1,128)}, u32[]{:S(2)}, u32[]{:S(2)}) async-start(f32[32,3,1,40]{3,2,1,0:T(1,128)} %copy.670), calls=%async_computation.3 | async-start | bytes 98304 | tf_op jit(solution)/shard_map/all_to_all | solution.py:101
  258.3 32.3 %collective-permute-start.9 = (f32[8,3,1,128]{3,2,0,1:T(1,128)}, f32[8,3,1,128]{3,2,0,1:T(1,128)}, u32[]{:S(2)}, u32[]{:S(2)}) collective-permute-start(f32[8,3,1,128]{3,2,0,1:T(1,128)} %get-tuple-element.98), channel_id=1, source_target_pairs={{8,0},{16,8},{24,16},{9,1},{17,9},{25,17},{10,2},{18,10},{26,18},{... | collective-permute-start | bytes 36872 | tf_op jit(solution)/shard_map/ppermute | solution.py:17
  259.6 31.0 %collective-permute-start.8 = (f32[8,3,1,128]{3,2,0,1:T(1,128)}, f32[8,3,1,128]{3,2,0,1:T(1,128)}, u32[]{:S(2)}, u32[]{:S(2)}) collective-permute-start(f32[8,3,1,128]{3,2,0,1:T(1,128)} %get-tuple-element.97), channel_id=1, source_target_pairs={{0,8},{8,16},{16,24},{1,9},{9,17},{17,25},{2,10},{10,18},{18,26},{... | collective-permute-start | bytes 36872 | tf_op jit(solution)/shard_map/ppermute | solution.py:14
  286.7 11.1 %all-to-all-start.4 = ((f32[3,32,40]{2,0,1:T(4,128)}), f32[3,32,40]{2,0,1:T(4,128)}, u32[]{:S(2)}, u32[]{:S(2)}) async-start(f32[3,32,40]{2,0,1:T(4,128)} %bitcast.1128), calls=%async_computation.4 | async-start | bytes 131072 | tf_op jit(solution)/shard_map/all_to_all | solution.py:96
  292.6 71.2 %collective-permute-start.11 = (f32[8,3,18,1]{3,2,0,1:T(8,128)}, f32[8,3,18,1]{3,2,0,1:T(8,128)}, u32[]{:S(2)}, u32[]{:S(2)}) collective-permute-start(f32[8,3,18,1]{3,2,0,1:T(8,128)} %get-tuple-element.53), channel_id=1, source_target_pairs={{1,0},{2,1},{3,2},{4,3},{5,4},{6,5},{7,6},{9,8},{10,9},{11,10},{12... | collective-permute-start | bytes 5192 | tf_op jit(solution)/shard_map/ppermute | solution.py:17
  293.8 69.9 %collective-permute-start.10 = (f32[8,3,18,1]{3,2,0,1:T(8,128)}, f32[8,3,18,1]{3,2,0,1:T(8,128)}, u32[]{:S(2)}, u32[]{:S(2)}) collective-permute-start(f32[8,3,18,1]{3,2,0,1:T(8,128)} %get-tuple-element.52), channel_id=1, source_target_pairs={{0,1},{1,2},{2,3},{3,4},{4,5},{5,6},{6,7},{8,9},{9,10},{10,11},{11... | collective-permute-start | bytes 5192 | tf_op jit(solution)/shard_map/ppermute | solution.py:14
  329.7 13.2 %all-to-all-start.5 = ((f32[32,3,1,40]{3,2,1,0:T(1,128)}), f32[32,3,1,40]{3,2,1,0:T(1,128)}, u32[]{:S(2)}, u32[]{:S(2)}) async-start(f32[32,3,1,40]{3,2,1,0:T(1,128)} %copy.691), calls=%async_computation.5 | async-start | bytes 98304 | tf_op jit(solution)/shard_map/all_to_all | solution.py:101
  415.1 32.3 %collective-permute-start.13 = (f32[8,3,1,128]{3,2,0,1:T(1,128)}, f32[8,3,1,128]{3,2,0,1:T(1,128)}, u32[]{:S(2)}, u32[]{:S(2)}) collective-permute-start(f32[8,3,1,128]{3,2,0,1:T(1,128)} %get-tuple-element.85), channel_id=1, source_target_pairs={{8,0},{16,8},{24,16},{9,1},{17,9},{25,17},{10,2},{18,10},{26,18},{... | collective-permute-start | bytes 36872 | tf_op jit(solution)/shard_map/ppermute | solution.py:17
  416.4 31.0 %collective-permute-start.12 = (f32[8,3,1,128]{3,2,0,1:T(1,128)}, f32[8,3,1,128]{3,2,0,1:T(1,128)}, u32[]{:S(2)}, u32[]{:S(2)}) collective-permute-start(f32[8,3,1,128]{3,2,0,1:T(1,128)} %get-tuple-element.84), channel_id=1, source_target_pairs={{0,8},{8,16},{16,24},{1,9},{9,17},{17,25},{2,10},{10,18},{18,26},{... | collective-permute-start | bytes 36872 | tf_op jit(solution)/shard_map/ppermute | solution.py:14
  443.5 11.3 %all-to-all-start.6 = ((f32[3,32,40]{2,0,1:T(4,128)}), f32[3,32,40]{2,0,1:T(4,128)}, u32[]{:S(2)}, u32[]{:S(2)}) async-start(f32[3,32,40]{2,0,1:T(4,128)} %bitcast.1129), calls=%async_computation.6 | async-start | bytes 131072 | tf_op jit(solution)/shard_map/all_to_all | solution.py:96
  449.3 71.3 %collective-permute-start.15 = (f32[8,3,18,1]{3,2,0,1:T(8,128)}, f32[8,3,18,1]{3,2,0,1:T(8,128)}, u32[]{:S(2)}, u32[]{:S(2)}) collective-permute-start(f32[8,3,18,1]{3,2,0,1:T(8,128)} %get-tuple-element.51), channel_id=1, source_target_pairs={{1,0},{2,1},{3,2},{4,3},{5,4},{6,5},{7,6},{9,8},{10,9},{11,10},{12... | collective-permute-start | bytes 5192 | tf_op jit(solution)/shard_map/ppermute | solution.py:17
  450.6 70.0 %collective-permute-start.14 = (f32[8,3,18,1]{3,2,0,1:T(8,128)}, f32[8,3,18,1]{3,2,0,1:T(8,128)}, u32[]{:S(2)}, u32[]{:S(2)}) collective-permute-start(f32[8,3,18,1]{3,2,0,1:T(8,128)} %get-tuple-element.50), channel_id=1, source_target_pairs={{0,1},{1,2},{2,3},{3,4},{4,5},{5,6},{6,7},{8,9},{9,10},{10,11},{11... | collective-permute-start | bytes 5192 | tf_op jit(solution)/shard_map/ppermute | solution.py:14
  486.7 13.1 %all-to-all-start.7 = ((f32[32,3,1,40]{3,2,1,0:T(1,128)}), f32[32,3,1,40]{3,2,1,0:T(1,128)}, u32[]{:S(2)}, u32[]{:S(2)}) async-start(f32[32,3,1,40]{3,2,1,0:T(1,128)} %copy.711), calls=%async_computation.7 | async-start | bytes 98304 | tf_op jit(solution)/shard_map/all_to_all | solution.py:101
  566.6 26.4 %collective-permute-start.17 = (f32[8,3,1,128]{3,2,0,1:T(1,128)S(1)}, f32[8,3,1,128]{3,2,0,1:T(1,128)S(1)}, u32[]{:S(2)}, u32[]{:S(2)}) collective-permute-start(f32[8,3,1,128]{3,2,0,1:T(1,128)S(1)} %get-tuple-element.74), channel_id=1, source_target_pairs={{8,0},{16,8},{24,16},{9,1},{17,9},{25,17},{10,2},{18,10},{26,18},{... | collective-permute-start | bytes 36872 | tf_op jit(solution)/shard_map/ppermute | solution.py:17
  567.9 25.1 %collective-permute-start.16 = (f32[8,3,1,128]{3,2,0,1:T(1,128)S(1)}, f32[8,3,1,128]{3,2,0,1:T(1,128)S(1)}, u32[]{:S(2)}, u32[]{:S(2)}) collective-permute-start(f32[8,3,1,128]{3,2,0,1:T(1,128)S(1)} %get-tuple-element.73), channel_id=1, source_target_pairs={{0,8},{8,16},{16,24},{1,9},{9,17},{17,25},{2,10},{10,18},{18,26},{... | collective-permute-start | bytes 36872 | tf_op jit(solution)/shard_map/ppermute | solution.py:14
  573.5 35.5 %copy-start.23 = (s32[2048]{0:T(1024)S(1)}, s32[2048]{0:T(1024)}, u32[]{:S(2)}) copy-start(s32[2048]{0:T(1024)} %copy-done.22) | copy-start | bytes 24580
  588.6 11.7 %all-to-all-start.8 = ((f32[3,32,40]{2,0,1:T(4,128)}), f32[3,32,40]{2,0,1:T(4,128)S(1)}, u32[]{:S(2)}, u32[]{:S(2)}) async-start(f32[3,32,40]{2,0,1:T(4,128)} %bitcast.286), calls=%async_computation.8 | async-start | bytes 131072 | tf_op jit(solution)/shard_map/all_to_all | solution.py:96
  594.0 54.8 %collective-permute-start.19 = (f32[8,3,18,1]{3,2,0,1:T(8,128)}, f32[8,3,18,1]{3,2,0,1:T(8,128)}, u32[]{:S(2)}, u32[]{:S(2)}) collective-permute-start(f32[8,3,18,1]{3,2,0,1:T(8,128)} %get-tuple-element.49), channel_id=1, source_target_pairs={{1,0},{2,1},{3,2},{4,3},{5,4},{6,5},{7,6},{9,8},{10,9},{11,10},{12... | collective-permute-start | bytes 5192 | tf_op jit(solution)/shard_map/ppermute | solution.py:17
  595.3 53.5 %collective-permute-start.18 = (f32[8,3,18,1]{3,2,0,1:T(8,128)}, f32[8,3,18,1]{3,2,0,1:T(8,128)}, u32[]{:S(2)}, u32[]{:S(2)}) collective-permute-start(f32[8,3,18,1]{3,2,0,1:T(8,128)} %get-tuple-element.48), channel_id=1, source_target_pairs={{0,1},{1,2},{2,3},{3,4},{4,5},{5,6},{6,7},{8,9},{9,10},{10,11},{11... | collective-permute-start | bytes 5192 | tf_op jit(solution)/shard_map/ppermute | solution.py:14
  617.1 12.2 %all-to-all-start.9 = ((f32[32,3,1,40]{3,2,1,0:T(1,128)}), f32[32,3,1,40]{3,2,1,0:T(1,128)S(1)}, u32[]{:S(2)}, u32[]{:S(2)}) async-start(f32[32,3,1,40]{3,2,1,0:T(1,128)} %copy.731), calls=%async_computation.9 | async-start | bytes 98304 | tf_op jit(solution)/shard_map/all_to_all | solution.py:101
  630.5 60.7 %copy-start.27 = (f32[8,3,16,128]{3,2,0,1:T(8,128)S(1)}, f32[8,3,16,128]{3,2,0,1:T(8,128)}, u32[]{:S(2)}) copy-start(f32[8,3,16,128]{3,2,0,1:T(8,128)} %copy-done.26) | copy-start | bytes 589828
  630.5 60.7 %copy-start.29 = (f32[8,3,16,128]{3,2,0,1:T(8,128)S(1)}, f32[8,3,16,128]{3,2,0,1:T(8,128)}, u32[]{:S(2)}) copy-start(f32[8,3,16,128]{3,2,0,1:T(8,128)} %copy-done.28) | copy-start | bytes 589828
  630.5 60.7 %copy-start.31 = (f32[8,3,16,128]{3,2,0,1:T(8,128)S(1)}, f32[8,3,16,128]{3,2,0,1:T(8,128)}, u32[]{:S(2)}) copy-start(f32[8,3,16,128]{3,2,0,1:T(8,128)} %copy-done.30) | copy-start | bytes 589828
  630.5 60.7 %copy-start.33 = (f32[8,3,16,128]{3,2,0,1:T(8,128)S(1)}, f32[8,3,16,128]{3,2,0,1:T(8,128)}, u32[]{:S(2)}) copy-start(f32[8,3,16,128]{3,2,0,1:T(8,128)} %copy-done.32) | copy-start | bytes 589828
  630.5 60.7 %copy-start.37 = (f32[8,3,16,128]{3,2,1,0:T(8,128)S(1)}, f32[8,3,16,128]{3,2,1,0:T(8,128)}, u32[]{:S(2)}) copy-start(f32[8,3,16,128]{3,2,1,0:T(8,128)} %param.12) | copy-start | bytes 589828
  643.5 47.8 %copy-start.6 = (bf16[8,3,1,16,128]{4,3,2,1,0:T(8,128)(2,1)S(1)}, bf16[8,3,1,16,128]{4,3,2,1,0:T(8,128)(2,1)}, u32[]{:S(2)}) copy-start(bf16[8,3,1,16,128]{4,3,2,1,0:T(8,128)(2,1)} %copy-done.5) | copy-start | bytes 294916
  643.5 47.8 %copy-start.8 = (bf16[8,3,1,16,128]{4,3,2,1,0:T(8,128)(2,1)S(1)}, bf16[8,3,1,16,128]{4,3,2,1,0:T(8,128)(2,1)}, u32[]{:S(2)}) copy-start(bf16[8,3,1,16,128]{4,3,2,1,0:T(8,128)(2,1)} %copy-done.7) | copy-start | bytes 294916
  643.5 47.8 %copy-start.10 = (bf16[8,3,1,16,128]{4,3,2,1,0:T(8,128)(2,1)S(1)}, bf16[8,3,1,16,128]{4,3,2,1,0:T(8,128)(2,1)}, u32[]{:S(2)}) copy-start(bf16[8,3,1,16,128]{4,3,2,1,0:T(8,128)(2,1)} %copy-done.9) | copy-start | bytes 294916
  691.5 25.7 %collective-permute-start.21 = (f32[8,3,1,128]{3,2,0,1:T(1,128)S(1)}, f32[8,3,1,128]{3,2,0,1:T(1,128)S(1)}, u32[]{:S(2)}, u32[]{:S(2)}) collective-permute-start(f32[8,3,1,128]{3,2,0,1:T(1,128)S(1)} %get-tuple-element.67), channel_id=1, source_target_pairs={{8,0},{16,8},{24,16},{9,1},{17,9},{25,17},{10,2},{18,10},{26,18},{... | collective-permute-start | bytes 36872 | tf_op jit(solution)/shard_map/ppermute | solution.py:17
  692.8 24.4 %collective-permute-start.20 = (f32[8,3,1,128]{3,2,0,1:T(1,128)S(1)}, f32[8,3,1,128]{3,2,0,1:T(1,128)S(1)}, u32[]{:S(2)}, u32[]{:S(2)}) collective-permute-start(f32[8,3,1,128]{3,2,0,1:T(1,128)S(1)} %get-tuple-element.66), channel_id=1, source_target_pairs={{0,8},{8,16},{16,24},{1,9},{9,17},{17,25},{2,10},{10,18},{18,26},{... | collective-permute-start | bytes 36872 | tf_op jit(solution)/shard_map/ppermute | solution.py:14
  712.8 11.8 %all-to-all-start.10 = ((f32[3,32,40]{2,0,1:T(4,128)}), f32[3,32,40]{2,0,1:T(4,128)S(1)}, u32[]{:S(2)}, u32[]{:S(2)}) async-start(f32[3,32,40]{2,0,1:T(4,128)} %bitcast.337), calls=%async_computation.10 | async-start | bytes 131072 | tf_op jit(solution)/shard_map/all_to_all | solution.py:96
  718.1 53.6 %collective-permute-start.23 = (f32[8,3,18,1]{3,2,0,1:T(8,128)}, f32[8,3,18,1]{3,2,0,1:T(8,128)}, u32[]{:S(2)}, u32[]{:S(2)}) collective-permute-start(f32[8,3,18,1]{3,2,0,1:T(8,128)} %get-tuple-element.47), channel_id=1, source_target_pairs={{1,0},{2,1},{3,2},{4,3},{5,4},{6,5},{7,6},{9,8},{10,9},{11,10},{12... | collective-permute-start | bytes 5192 | tf_op jit(solution)/shard_map/ppermute | solution.py:17
  719.4 52.3 %collective-permute-start.22 = (f32[8,3,18,1]{3,2,0,1:T(8,128)}, f32[8,3,18,1]{3,2,0,1:T(8,128)}, u32[]{:S(2)}, u32[]{:S(2)}) collective-permute-start(f32[8,3,18,1]{3,2,0,1:T(8,128)} %get-tuple-element.46), channel_id=1, source_target_pairs={{0,1},{1,2},{2,3},{3,4},{4,5},{5,6},{6,7},{8,9},{9,10},{10,11},{11... | collective-permute-start | bytes 5192 | tf_op jit(solution)/shard_map/ppermute | solution.py:14
  741.2 12.1 %all-to-all-start.11 = ((f32[32,3,1,40]{3,2,1,0:T(1,128)}), f32[32,3,1,40]{3,2,1,0:T(1,128)S(1)}, u32[]{:S(2)}, u32[]{:S(2)}) async-start(f32[32,3,1,40]{3,2,1,0:T(1,128)} %copy.738), calls=%async_computation.11 | async-start | bytes 98304 | tf_op jit(solution)/shard_map/all_to_all | solution.py:101
  (61 other events, 871.1 us)
